TPU v7x, 256 devices: a whole 4x4x8 slice. The times are simulated.
256 devices in a mesh: tm: 32 (over z, y_hi, core), space: 8 (over y_lo, x).
Axes of the slice: x: 4, y: 4 (y_hi: 2, y_lo: 2; y = y_hi * 2 + y_lo), z: 8, core: 2. Of those that a mesh axis runs over, the one named last changes fastest.
Arguments:
- model: float32 [32, 8192, 1024], P('tm', 'space'), may hold values from -6 to 6
- kernels: float32 [3, 600, 8192], P(None, None, ('space', 'tm')), may hold values from -0.0390625 to 0.0390625
Outputs:
- data: float32 [32, 600, 1024], P('tm', None, 'space')
All inputs are finite; a program needn't handle non-finite values.
Results may differ from a plain program's by a relative error of at most 0.0003.
Values sent between devices are 32-bit elements; how exact they have to be, the bound alone decides.
A program may use at most 64 MiB of HBM per device.

v0:
```python
import jax
import jax.numpy as jnp
from jax import lax
from jax.sharding import PartitionSpec as P


def passed_along(block, axis, distance):
    devices = range(lax.axis_size(axis))
    route = [(i - distance, i) for i in devices if i - distance in devices]
    return lax.ppermute(block, axis, route)


def on_device(model, kernels):
    local_model = model[0]
    lag_count = kernels.shape[0]
    products = jnp.einsum(
        "lsp,pc->lsc",
        lax.all_gather(kernels, "tm", axis=2, tiled=True),
        local_model,
        precision=lax.Precision.HIGHEST,
        preferred_element_type=jnp.float32,
    )
    running = products[lag_count - 1]
    for lag_index in range(lag_count - 2, -1, -1):
        running = passed_along(running, "tm", 1) + products[lag_index]
    result = lax.psum_scatter(running, "space", scatter_dimension=1, tiled=True)
    return result[None]


def solution(mesh):
    return jax.shard_map(
        on_device,
        mesh=mesh,
        in_specs=(P("tm", "space", None), P(None, None, ("space", "tm"))),
        out_specs=P("tm", None, "space"),
        check_vma=False,
    )
```

profile of v0, /device:TPU:32, one launch (start us, length us, event | category | flops | bytes accessed | tf_op | source)
XLA Modules:
  0.0 261.7 jit_solution(11356863142729187960)
XLA Ops:
  6.5 0.0 all-gather.2.cloned.1.call-start
  6.5 0.7 all-gather.2.cloned.1.call-update
  7.3 0.0 reduce-scatter.2.cloned.1.call-start
  7.3 104.9 %all-gather.2.cloned.1.call-done = f32[3,600,1024]{1,2,0:T(8,128)} async-done(((f32[3,600,32]{1,2,0:T(8,128)}), f32[3,600,1024]{1,2,0:T(8,128)}) %all-gather.2.cloned.1.call-update) | async-done | bytes 7372816 | tf_op jit(solution)/shard_map/all_gather | solution.py:18
  112.2 27.5 %fusion = f32[3,600,1024]{2,1,0:T(8,128)S(1)} fusion(f32[3,600,1024]{1,2,0:T(8,128)} %all-gather.2.cloned.1.call-done, f32[1,1024,1024]{2,1,0:T(8,128)} %param.2), kind=kOutput, calls=%fused_computation | convolution fusion | flops 22649241600 | bytes 18939904 | tf_op jit(solution)/shard_map/lsp,pc->lsc/dot_general | solution.py:16
  139.7 0.2 slice_bitcast_fusion.2
  139.9 2.2 collective-permute-start
  142.1 31.5 %collective-permute-done = f32[600,1024]{1,0:T(8,128)S(1)} collective-permute-done((f32[600,1024]{1,0:T(8,128)S(1)}, f32[600,1024]{1,0:T(8,128)S(1)}, u32[]{:S(2)}, u32[]{:S(2)}) %collective-permute-start) | collective-permute-done | bytes 2457632 | tf_op jit(solution)/shard_map/ppermute | solution.py:10
  173.5 0.5 fusion.3
  174.0 1.9 collective-permute-start.1
  175.9 31.7 %collective-permute-done.1 = f32[600,1024]{1,0:T(8,128)S(1)} collective-permute-done((f32[600,1024]{1,0:T(8,128)S(1)}, f32[600,1024]{1,0:T(8,128)S(1)}, u32[]{:S(2)}, u32[]{:S(2)}) %collective-permute-start.1) | collective-permute-done | bytes 2457632 | tf_op jit(solution)/shard_map/ppermute | solution.py:10
  207.6 1.9 fusion.2
  209.5 0.0 reduce-scatter.2.cloned.1.call-update
  209.6 45.3 %reduce-scatter.2.cloned.1.call-done = f32[600,128]{1,0:T(8,128)} async-done(((f32[600,1024]{1,0:T(8,128)}), f32[600,128]{1,0:T(8,128)}) %reduce-scatter.2.cloned.1.call-update) | async-done | bytes 307216 | tf_op jit(solution)/shard_map/reduce_scatter | solution.py:26
Async XLA Ops:
  6.5 105.7 %all-gather.2.cloned.1.call-start = ((), (), s32[]{:S(2)}) async-start(), calls=%async_computation.1 | async-start | bytes 8110080 | tf_op jit(solution)/shard_map/all_gather | solution.py:18
  7.3 247.6 %reduce-scatter.2.cloned.1.call-start = ((), (), s32[]{:S(2)}) async-start(), calls=%async_computation.2 | async-start | bytes 2764800 | tf_op jit(solution)/shard_map/reduce_scatter | solution.py:26
  139.9 33.6 %collective-permute-start = (f32[600,1024]{1,0:T(8,128)S(1)}, f32[600,1024]{1,0:T(8,128)S(1)}, u32[]{:S(2)}, u32[]{:S(2)}) collective-permute-start(f32[600,1024]{1,0:T(8,128)S(1)} %slice_bitcast_fusion.2), channel_id=1, source_target_pairs={{0,8},{8,16},{16,24},{24,32},{32,40},{40,48},{48,56},{56,64},{64,7... | collective-permute-start | bytes 7372808 | tf_op jit(solution)/shard_map/ppermute | solution.py:10
  174.0 33.6 %collective-permute-start.1 = (f32[600,1024]{1,0:T(8,128)S(1)}, f32[600,1024]{1,0:T(8,128)S(1)}, u32[]{:S(2)}, u32[]{:S(2)}) collective-permute-start(f32[600,1024]{1,0:T(8,128)S(1)} %fusion.3), channel_id=1, source_target_pairs={{0,8},{8,16},{16,24},{24,32},{32,40},{40,48},{48,56},{56,64},{64,7... | collective-permute-start | bytes 7372808 | tf_op jit(solution)/shard_map/ppermute | solution.py:10
Sparse Core Ops, SparseCore 0:
  10.1 102.0 all-gather.1
  209.7 45.1 reduce-scatter.1
where the time goes:
time: 262 us
  waiting for transfers between devices  214 us (82%)
  matrix products  27.5 us (10%)
  between operations  13.4 us (5%)
  starting transfers between devices  4.12 us (2%)
    all_gather x1, waiting for transfers between devices, on_device(): lax.all_gather(kernels, 'tm', axis=2, tiled=True)  105 us
    ppermute x2, waiting for transfers between devices, passed_along(): return lax.ppermute(block, axis, route)  63.1 us
    reduce_scatter x1, waiting for transfers between devices, on_device(): result = lax.psum_scatter(running, 'space', scatter_dimension=1, tiled=True)  45.3 us
    dot_general x1, matrix products, on_device(): jnp.einsum('lsp,pc->lsc', lax.all_gather(kernels, 'tm', axis=2, tiled=Tru...  27.5 us
  transfers between devices with their start and end apart: 4, of which 4 were waited for; matrix products, arithmetic and copies ran while one was open for 0% of the time, Pallas kernels for 0%

commit v1 on v0

v1 whole, which is shorter than its diff:
```python
import functools

import jax
import jax.numpy as jnp
from jax import lax
from jax.experimental import pallas as pl
from jax.experimental.pallas import tpu as pltpu
from jax.sharding import PartitionSpec as P

NZ, NX = 8, 4
CHUNKS, ROWS = 5, 120
LAGS = 3
MESH = pl.DeviceIdType.MESH
F32, BF16 = jnp.float32, jnp.bfloat16


def kernel(
    m_hbm, k_ref, out_ref,
    m_buf, k_pad, kbuf, kt_hi, kt_lo, w_hi, w_lo, pbuf, p1s, p1r, r1, r2, r3,
    m_sem, ky_s, ky_r, kz_s, kz_r, kf_s, kf_r, p1_s, p1_rs, r1_s, r1_r, r2_s, r2_r, r3_s, r3_r,
):
    tm, space = lax.axis_index("tm"), lax.axis_index("space")
    z, yh, c = tm // 4, (tm // 2) % 2, tm % 2
    yl, x = space // NX, space % NX

    def at_z(step):
        return ((z + step + NZ) % NZ * 4 + yh * 2 + c, space)

    def at_x(step):
        return (tm, yl * NX + (x + step + NX) % NX)

    other_yh = (z * 4 + (1 - yh) * 2 + c, space)
    other_core = (z * 4 + yh * 2 + (1 - c), space)
    other_yl = (tm, (1 - yl) * NX + x)
    later, earlier = (tm + 2) % 32, (tm + 30) % 32
    has_later, has_earlier = tm < 30, tm >= 2

    barrier = pltpu.get_barrier_semaphore()
    greeted = [
        at_z(1), at_z(-1), at_x(1), at_x(-1), other_yh, other_core, other_yl,
        (later, space), (later, other_yl[1]), (earlier, space), (earlier, other_yl[1]),
    ]
    for device in greeted:
        pl.semaphore_signal(barrier, inc=1, device_id=device, device_id_type=MESH)

    def load_model(i):
        rows = pl.ds(i * 256, 256)
        return pltpu.make_async_copy(m_hbm.at[rows], m_buf.at[rows], m_sem.at[i])

    for i in range(4):
        load_model(i).start()
    k_pad[...] = jnp.zeros_like(k_pad)
    for lag in range(LAGS):
        k_pad[lag, :, 0:600] = k_ref[lag]
    for lag in range(LAGS):
        whole = k_pad[lag]
        for j in range(CHUNKS):
            moved = whole if j == 0 else pltpu.roll(whole, 640 - ROWS * j, 1)
            kbuf[j, lag, c * NZ + z, yh] = moved[:, 0:128]
    pl.semaphore_wait(barrier, len(greeted))

    def remote(src, dst, send, recv, device):
        return pltpu.make_async_remote_copy(
            src_ref=src, dst_ref=dst, send_sem=send, recv_sem=recv, device_id=device, device_id_type=MESH
        )

    def over_yh(j, half):
        block = kbuf.at[j, :, c * NZ + z, half]
        return remote(block, block, ky_s.at[j], ky_r.at[j], other_yh)

    def over_z(j, hop, direction, source):
        sign = 1 - 2 * direction
        index = c * NZ + (z - sign * (source) + NZ) % NZ
        block = kbuf.at[j, :, index] if hop < 4 else kbuf.at[j, :, index, direction]
        return remote(block, block, kz_s.at[j, direction, hop - 1], kz_r.at[j, direction, hop - 1], at_z(sign))

    def send_z(j, hop, direction):
        return over_z(j, hop, direction, hop - 1)

    def recv_z(j, hop, direction):
        return over_z(j, hop, direction, hop)

    def to_core(j, core, hop, direction):
        sign = 1 - 2 * direction
        index = core * NZ + (z - sign * hop + NZ) % NZ
        block = kbuf.at[j, :, index] if hop < 4 else kbuf.at[j, :, index, direction]
        slot = 0 if hop == 0 else 2 * hop - 1 + direction
        return remote(block, block, kf_s.at[j, slot], kf_r.at[j, slot], other_core)

    hops = [(0, 0)] + [(hop, direction) for hop in (1, 2, 3, 4) for direction in (0, 1)]

    def advance(j, hop):
        if hop == 1:
            over_yh(j, 1 - yh).wait_recv()
            for direction in (0, 1):
                send_z(j, 1, direction).start()
            to_core(j, c, 0, 0).start()
        else:
            for direction in (0, 1):
                recv_z(j, hop - 1, direction).wait_recv()
                if hop <= 4:
                    send_z(j, hop, direction).start()
                to_core(j, c, hop - 1, direction).start()

    def swap_core(j, slot):
        return remote(p1s.at[j, slot], p1r.at[j, slot], p1_s.at[j, slot], p1_rs.at[j, slot], other_core)

    def first_x(j, direction):
        return remote(
            pbuf.at[j, 0, direction], r1.at[j, direction], r1_s.at[j, direction], r1_r.at[j, direction],
            at_x(1 - 2 * direction),
        )

    def second_x(j, direction):
        return remote(
            pbuf.at[j, 1 + direction], r2.at[j, direction], r2_s.at[j, direction], r2_r.at[j, direction],
            at_x(1 - 2 * direction),
        )

    def last(j, which):
        src = (pbuf.at[j, 3, 1 - yl, 0], pbuf.at[j, 3, yl, 1], pbuf.at[j, 3, 1 - yl, 1])[which]
        device = (other_yl, (later, space), (later, other_yl[1]))[which]
        return remote(src, r3.at[j, which], r3_s.at[j, which], r3_r.at[j, which], device)

    def transpose_chunk(j):
        def block(b, carry):
            for lag in range(LAGS):
                part = kbuf[j, lag, pl.ds(2 * b, 2)].reshape(128, 128).T
                high = part.astype(BF16)
                low = (part - high.astype(F32)).astype(BF16)
                columns = pl.ds(pl.multiple_of(b * 128, 128), 128)
                kt_hi[lag * 128 : (lag + 1) * 128, columns] = high
                kt_lo[lag * 128 : (lag + 1) * 128, columns] = low
            return carry

        lax.fori_loop(0, NZ, block, 0)

    def multiply(j, slot):
        to = (x + (2, 1, 3, 0)[slot]) % NX
        wide = w_hi[to]
        acc = jnp.dot(kt_hi[...], wide, preferred_element_type=F32)
        acc = acc + jnp.dot(kt_lo[...], wide, preferred_element_type=F32)
        acc = acc + jnp.dot(kt_hi[...], w_lo[to], preferred_element_type=F32)
        for half in (0, 1):
            lanes = slice(half * 128, half * 128 + 128)
            pbuf[j, slot, half, 0] = acc[0:ROWS, lanes]
            p1s[j, slot, half] = acc[128 : 128 + ROWS, lanes]
            pbuf[j, slot, half, 1] = acc[256 : 256 + ROWS, lanes]
        swap_core(j, slot).start()

    def combine(j, slot):
        swap_core(j, slot).wait_recv()
        for half in (0, 1):
            pbuf[j, slot, half, 1 - c] += p1r[j, slot, half]

    for j in range(CHUNKS):
        over_yh(j, yh).start()

    for i in range(4):
        load_model(i).wait()

    def split_rows(t, carry):
        rows = m_buf[pl.ds(pl.multiple_of(t * 32, 32), 32), :]
        high = rows.astype(BF16)
        low = (rows - high.astype(F32)).astype(BF16)
        to = pl.ds(pl.multiple_of(((t % 2) * NZ + t // 4) * 64 + (t // 2) % 2 * 32, 32), 32)
        for d in range(NX):
            for half in (0, 1):
                lanes = slice(half * 128, half * 128 + 128)
                columns = slice(half * 512 + d * 128, half * 512 + d * 128 + 128)
                w_hi[d, to, lanes] = high[:, columns]
                w_lo[d, to, lanes] = low[:, columns]
        return carry

    lax.fori_loop(0, 32, split_rows, 0)

    def iteration(i, carry):
        def on(offset):
            return (i - offset >= 0) & (i - offset < CHUNKS)

        @pl.when(on(0))
        def _():
            advance(i, 1)

        @pl.when(on(2))
        def _():
            advance(i - 2, 5)

        @pl.when(on(1))
        def _():
            advance(i - 1, 3)

        @pl.when(on(2))
        def _():
            j = i - 2
            for hop, direction in hops:
                to_core(j, 1 - c, hop, direction).wait_recv()
            transpose_chunk(j)
            multiply(j, 0)

        @pl.when(on(0))
        def _():
            advance(i, 2)

        @pl.when(on(2))
        def _():
            j = i - 2
            multiply(j, 1)
            combine(j, 0)
            for direction in (0, 1):
                first_x(j, direction).start()

        @pl.when(on(1))
        def _():
            advance(i - 1, 4)

        @pl.when(on(2))
        def _():
            j = i - 2
            multiply(j, 2)
            combine(j, 1)

        @pl.when(on(3))
        def _():
            j = i - 3
            for direction in (0, 1):
                first_x(j, direction).wait_recv()
                pbuf[j, 1 + direction, direction] += r1[j, direction]
                second_x(j, direction).start()

        @pl.when(on(2))
        def _():
            j = i - 2
            multiply(j, 3)
            combine(j, 2)
            combine(j, 3)

        @pl.when(on(4))
        def _():
            j = i - 4
            for direction in (0, 1):
                second_x(j, direction).wait_recv()
            pbuf[j, 3] = pbuf[j, 3] + r2[j, 0] + r2[j, 1]
            last(j, 0).start()

            @pl.when(has_later)
            def _():
                last(j, 1).start()
                last(j, 2).start()

        @pl.when(on(5))
        def _():
            j = i - 5
            last(j, 0).wait_recv()
            out_ref[j] = pbuf[j, 3, yl, 0] + r3[j, 0]

            @pl.when(has_earlier)
            def _():
                last(j, 1).wait_recv()
                last(j, 2).wait_recv()
                out_ref[j] = out_ref[j] + r3[j, 1] + r3[j, 2]

        return carry

    lax.fori_loop(0, CHUNKS + 5, iteration, 0)

    def drain(j, carry):
        over_yh(j, yh).wait_send()
        for direction in (0, 1):
            for hop in (1, 2, 3, 4):
                send_z(j, hop, direction).wait_send()
            first_x(j, direction).wait_send()
            second_x(j, direction).wait_send()
        for hop, direction in hops:
            to_core(j, c, hop, direction).wait_send()
        for slot in range(4):
            swap_core(j, slot).wait_send()
        last(j, 0).wait_send()

        @pl.when(has_later)
        def _():
            last(j, 1).wait_send()
            last(j, 2).wait_send()

        return carry

    lax.fori_loop(0, CHUNKS, drain, 0)


def on_device(model, kernels):
    dma = pltpu.SemaphoreType.DMA
    vmem = pltpu.VMEM
    result = pl.pallas_call(
        kernel,
        out_shape=jax.ShapeDtypeStruct((CHUNKS, ROWS, 128), F32),
        in_specs=[pl.BlockSpec(memory_space=pl.ANY), pl.BlockSpec(memory_space=pltpu.VMEM)],
        out_specs=pl.BlockSpec(memory_space=pltpu.VMEM),
        scratch_shapes=[
            vmem((1024, 1024), F32),
            vmem((LAGS, 32, 640), F32),
            vmem((CHUNKS, LAGS, 2 * NZ, 2, 32, 128), F32),
            vmem((LAGS * 128, 1024), BF16),
            vmem((LAGS * 128, 1024), BF16),
            vmem((NX, 1024, 256), BF16),
            vmem((NX, 1024, 256), BF16),
            vmem((CHUNKS, 4, 2, 2, ROWS, 128), F32),
            vmem((CHUNKS, 4, 2, ROWS, 128), F32),
            vmem((CHUNKS, 4, 2, ROWS, 128), F32),
            vmem((CHUNKS, 2, 2, ROWS, 128), F32),
            vmem((CHUNKS, 2, 2, 2, ROWS, 128), F32),
            vmem((CHUNKS, 3, ROWS, 128), F32),
            dma((4,)),
            dma((CHUNKS,)), dma((CHUNKS,)),
            dma((CHUNKS, 2, 4)), dma((CHUNKS, 2, 4)),
            dma((CHUNKS, 9)), dma((CHUNKS, 9)),
            dma((CHUNKS, 4)), dma((CHUNKS, 4)),
            dma((CHUNKS, 2)), dma((CHUNKS, 2)),
            dma((CHUNKS, 2)), dma((CHUNKS, 2)),
            dma((CHUNKS, 3)), dma((CHUNKS, 3)),
        ],
        compiler_params=pltpu.CompilerParams(
            collective_id=0, has_side_effects=True, vmem_limit_bytes=60 * 1024 * 1024
        ),
        name="toeplitz",
    )(model[0], jnp.swapaxes(kernels, 1, 2))
    return result.reshape(1, CHUNKS * ROWS, 128)


def solution(mesh):
    return jax.shard_map(
        on_device,
        mesh=mesh,
        in_specs=(P("tm", "space", None), P(None, None, ("space", "tm"))),
        out_specs=P("tm", None, "space"),
        check_vma=False,
    )
```

time: 262 us -> 97.6 us (0.37)
  waiting for transfers between devices: 214 us -> 0 us
  Pallas kernels: 0 us -> 95.7 us
  matrix products: 27.5 us -> 0 us
  between operations: 13.4 us -> 0.01 us
  starting transfers between devices: 4.12 us -> 0 us
    all_gather x1 -> x0, waiting for transfers between devices: 105 us -> none  [on_device(): lax.all_gather(kernels, 'tm', axis=2, tiled=True)]
    pallas_call x0 -> x1, Pallas kernels: none -> 95.7 us  [on_device(): pl.pallas_call(kernel, out_shape=jax.ShapeDtypeStruct((CHUNKS, ROWS, 128)...]
    ppermute x2 -> x0, waiting for transfers between devices: 63.1 us -> none  [passed_along(): return lax.ppermute(block, axis, route)]
    reduce_scatter x1 -> x0, waiting for transfers between devices: 45.3 us -> none  [on_device(): result = lax.psum_scatter(running, 'space', scatter_dimension=1, tiled=True)]
    dot_general x1 -> x0, matrix products: 27.5 us -> none  [on_device(): jnp.einsum('lsp,pc->lsc', lax.all_gather(kernels, 'tm', axis=2, tiled=Tru...]
    ppermute x2 -> x0, starting transfers between devices: 4.08 us -> none  [passed_along(): return lax.ppermute(block, axis, route)]
  transfers between devices with their start and end apart: 4 -> 0, of which waited for: 4 -> 0; matrix products, arithmetic and copies ran while one was open for 0% -> 0% of each run, Pallas kernels for 0% -> 0%
where the time goes in v1:
time: 97.6 us; the launch traced here: 97.4 us
  Pallas kernels  95.7 us (98%)
  local copies, waits for them, and re-layouts  1.7 us (2%)
    pallas_call x1, Pallas kernels, on_device(): pl.pallas_call(kernel, out_shape=jax.ShapeDtypeStruct((CHUNKS, ROWS, 128)...  95.7 us

profile of v1, /device:TPU:32, one launch (start us, length us, event | category | flops | bytes accessed | tf_op | source)
XLA Modules:
  0.0 97.4 jit_solution(3771138713981699441)
XLA Ops:
  0.0 95.7 %toeplitz.1 = f32[5,120,128]{2,1,0:T(8,128)} custom-call(f32[1024,1024]{1,0:T(8,128)} %bitcast.3, f32[3,32,600]{2,1,0:T(8,128)} %bitcast.5), custom_call_target="tpu_custom_call" | custom-call | tf_op jit(solution)/shard_map/toeplitz/pallas_call | solution.py:293
  95.7 1.7 %copy.4 = f32[1,600,128]{2,1,0:T(8,128)} copy(f32[1,600,128]{2,1,0:T(8,128)} %bitcast.4) | data formatting | bytes 614400

commit v2 on v0

v2 whole, which is shorter than its diff:
```python
import functools

import jax
import jax.numpy as jnp
from jax import lax
from jax.experimental import pallas as pl
from jax.experimental.pallas import tpu as pltpu
from jax.sharding import PartitionSpec as P

NZ, NX = 8, 4
LAGS, UNIT, UNITS = 3, 40, 15
MESH = pl.DeviceIdType.MESH
F32, BF16 = jnp.float32, jnp.bfloat16

SIZES = (1, 1, 2, 1, 3, 1, 3, 2, 1)
GATHER = "gcccgcccc"
REDUCE = "ddxddyyxx"
ORDER = (
    ("Y", 0), ("H1", 0), ("Y", 1), ("S", 0), ("Y", 2), ("Y", 3), ("Y", 4), ("H1", 4), ("Y", 5), ("H2", 0), ("H1", 1),
    ("Y", 6), ("H1", 2), ("Y", 7), ("Y", 8), ("H1", 3), ("H3", 0), ("H2", 1), ("H2", 4), ("H2", 2), ("H4", 0),
    ("H2", 3), ("H3", 1), ("H3", 4), ("H3", 2), ("H5", 0), ("H3", 3), ("H4", 1), ("H1", 5), ("H4", 4), ("H4", 2),
    ("F", 0), ("H1", 6), ("F", 1), ("T", 0), ("H4", 3), ("H5", 4), ("C0", 0), ("H2", 5), ("C1", 0), ("F", 2),
    ("C2", 0), ("H1", 7), ("C3", 0), ("T", 1), ("X0", 0), ("R1", 0), ("X1", 0), ("C0", 1), ("H2", 6), ("C1", 1),
    ("C2", 1), ("F", 3), ("X2", 0), ("R2", 0), ("X3", 0), ("C3", 1), ("F", 4), ("X0", 1), ("X1", 1), ("T", 2),
    ("H3", 5), ("R1", 1), ("X2", 1), ("X3", 1), ("C0", 2), ("H2", 7), ("C1", 2), ("R2", 1), ("C2", 2), ("H3", 6),
    ("C3", 2), ("R3", 0), ("X0", 2), ("R1", 2), ("X1", 2), ("T", 3), ("X2", 2), ("C0", 3), ("H4", 5), ("X3", 2),
    ("H1", 8), ("C1", 3), ("C2", 3), ("H3", 7), ("C3", 3), ("X0", 3), ("R1", 3), ("T", 4), ("H4", 6), ("R3", 1),
    ("X1", 3), ("X2", 3), ("R2", 3), ("F", 5), ("X3", 3), ("C0", 4), ("H2", 8), ("O", 0), ("R2", 2), ("C1", 4),
    ("H4", 7), ("C2", 4), ("F", 6), ("X0", 4), ("C3", 4), ("R3", 3), ("H3", 8), ("R1", 4), ("X1", 4), ("X2", 4),
    ("O", 1), ("T", 5), ("C0", 5), ("F", 7), ("C1", 5), ("C2", 5), ("C3", 5), ("R3", 2), ("X3", 4), ("X0", 5),
    ("T", 6), ("H4", 8), ("X1", 5), ("X2", 5), ("X3", 5), ("C0", 6), ("O", 3), ("R2", 4), ("C1", 6), ("C2", 6),
    ("X0", 6), ("C3", 6), ("F", 8), ("X1", 6), ("V0", 5), ("T", 7), ("O", 2), ("V1", 5), ("X2", 6), ("X3", 6),
    ("C0", 7), ("R1", 5), ("V2", 5), ("C1", 7), ("V3", 5), ("C2", 7), ("X0", 7), ("R1", 7), ("C3", 7), ("R3", 4),
    ("V0", 6), ("R1", 6), ("X1", 7), ("X2", 7), ("T", 8), ("C0", 8), ("X3", 7), ("R2", 5), ("C1", 8), ("C2", 8),
    ("C3", 8), ("V1", 6), ("X0", 8), ("R1", 8), ("D", 0), ("R2", 7), ("X1", 8), ("X2", 8), ("D", 1), ("X3", 8),
    ("D", 2), ("D", 3), ("V2", 6), ("R3", 5), ("R2", 6), ("V3", 6), ("R3", 7), ("R2", 8), ("R3", 6), ("O", 4),
    ("D", 4), ("O", 5), ("D", 5), ("R3", 8), ("O", 7), ("O", 6), ("D", 6), ("D", 7), ("O", 8), ("D", 8),
)
STARTS = tuple(sum(SIZES[:k]) for k in range(len(SIZES)))


def kernel(
    m_hbm, k_ref, out_ref,
    m_buf, k_pad, kbuf, kt_hi, kt_lo, w_hi, w_lo, pbuf, p1s, p1r, r0, r1, r2, r3, ry,
    m_sem, ky_s, ky_r, kz_s, kz_r, kf_s, kf_r, p1_s, p1_rs, r1_s, r1_r, r2_s, r2_r, r3_s, r3_r, ry_s, ry_r, kg_s, kg_r, kd_s, kd_r,
):
    tm, space = lax.axis_index("tm"), lax.axis_index("space")
    z, yh, c = tm // 4, (tm // 2) % 2, tm % 2
    yl, x = space // NX, space % NX

    def at_z(step):
        return ((z + step + NZ) % NZ * 4 + yh * 2 + c, space)

    def at_x(step):
        return (tm, yl * NX + (x + step + NX) % NX)

    other_yh = (z * 4 + (1 - yh) * 2 + c, space)
    other_core = (z * 4 + yh * 2 + (1 - c), space)
    other_yl = (tm, (1 - yl) * NX + x)
    later, earlier = (tm + 2) % 32, (tm + 30) % 32
    has_later, has_earlier = tm < 30, tm >= 2
    mine = c * NZ

    barrier = pltpu.get_barrier_semaphore()
    greeted = [
        (later, space), (later, other_yl[1]), (earlier, space), (earlier, other_yl[1]),
        at_z(1), at_z(-1), at_x(1), at_x(-1), other_yh, other_core, other_yl,
    ]
    if "d" in GATHER:
        greeted = [at_z(4), at_z(3), at_z(-3), at_z(2), at_z(-2)] + greeted
    if "d" in REDUCE:
        greeted = [at_x(2)] + greeted
    for device in greeted:
        pl.semaphore_signal(barrier, inc=1, device_id=device, device_id_type=MESH)

    def load_model(i):
        rows = pl.ds(i * 256, 256)
        return pltpu.make_async_copy(m_hbm.at[rows], m_buf.at[rows], m_sem.at[i])

    for i in range(4):
        load_model(i).start()

    k_pad[...] = jnp.zeros_like(k_pad)
    for lag in range(LAGS):
        k_pad[lag, :, 0:600] = k_ref[lag]
    lane = lax.broadcasted_iota(jnp.int32, (32, 128), 1)
    for u in range(UNITS):
        base = min(UNIT * u // 128 * 128, 384)
        parts = []
        for lag in range(LAGS):
            shift = (UNIT * lag - (UNIT * u - base)) % 256
            wide = k_pad[lag, :, base : base + 256]
            parts.append((pltpu.roll(wide, shift, 1) if shift else wide)[:, 0:128])
        tile = jnp.where(lane < UNIT, parts[0], jnp.where(lane < 2 * UNIT, parts[1], parts[2]))
        kbuf[u, mine + z, yh] = tile
    pl.semaphore_wait(barrier, len(greeted))

    def remote(src, dst, send, recv, device):
        return pltpu.make_async_remote_copy(
            src_ref=src, dst_ref=dst, send_sem=send, recv_sem=recv, device_id=device, device_id_type=MESH
        )

    def units(k):
        return pl.ds(STARTS[k], SIZES[k])

    def rows(k):
        return pl.ds(STARTS[k] * UNIT, SIZES[k] * UNIT)

    def over_yh(k, half):
        block = kbuf.at[units(k), mine + z, half]
        return remote(block, block, ky_s.at[k], ky_r.at[k], other_yh)

    def over_z(k, hop, direction, source):
        sign = 1 - 2 * direction
        index = mine + (z - sign * source + NZ) % NZ
        if GATHER[k] == "g":
            block = kbuf.at[units(k), index, yh]
        else:
            block = kbuf.at[units(k), index] if hop < 4 else kbuf.at[units(k), index, direction]
        return remote(block, block, kz_s.at[k, direction, hop - 1], kz_r.at[k, direction, hop - 1], at_z(sign))

    def ring_over_yh(k, hop, direction, half):
        index = mine + (z - (1 - 2 * direction) * hop + NZ) % NZ
        block = kbuf.at[units(k), index, half]
        return remote(block, block, kg_s.at[k, direction, hop - 1], kg_r.at[k, direction, hop - 1], other_yh)

    def straight(k, mirrored, step, source, half):
        block = kbuf.at[units(k), mine + (z - source + NZ) % NZ, half]
        return remote(block, block, kd_s.at[k, mirrored, step - 1], kd_r.at[k, mirrored, step - 1], at_z(step))

    def ring_hops(k):
        return [(hop, direction) for hop in (1, 2, 3) for direction in (0, 1)] + [(4, k % 2)]

    def to_core(k, core):
        block = kbuf.at[units(k), pl.ds(core * NZ, NZ)]
        return remote(block, block, kf_s.at[k], kf_r.at[k], other_core)

    def swap_core(k, slot):
        return remote(
            p1s.at[slot, :, rows(k)], p1r.at[slot, :, rows(k)], p1_s.at[k, slot], p1_rs.at[k, slot], other_core
        )

    def over_yl(k, slot):
        return remote(
            pbuf.at[slot, 1 - yl, :, rows(k)], ry.at[slot, :, rows(k)], ry_s.at[k, slot], ry_r.at[k, slot], other_yl
        )

    def first_x(k, direction):
        if REDUCE[k] == "y":
            src, dst = pbuf.at[0, yl, direction, rows(k)], r1.at[direction, 0, rows(k)]
        else:
            src, dst = pbuf.at[0, direction, :, rows(k)], r1.at[direction, :, rows(k)]
        return remote(src, dst, r1_s.at[k, direction], r1_r.at[k, direction], at_x(1 - 2 * direction))

    def far_x(k):
        return remote(pbuf.at[0, :, :, rows(k)], r0.at[:, :, rows(k)], r1_s.at[k, 0], r1_r.at[k, 0], at_x(2))

    def second_x(k, direction):
        if REDUCE[k] == "y":
            src, dst = pbuf.at[1 + direction, yl, :, rows(k)], r2.at[direction, 0, :, rows(k)]
        else:
            src, dst = pbuf.at[1 + direction, :, :, rows(k)], r2.at[direction, :, :, rows(k)]
        return remote(src, dst, r2_s.at[k, direction], r2_r.at[k, direction], at_x(1 - 2 * direction))

    def last(k, which):
        src = (
            pbuf.at[3, 1 - yl, 0, rows(k)], pbuf.at[3, yl, 1, rows(k)], pbuf.at[3, 1 - yl, 1, rows(k)]
        )[which]
        device = (other_yl, (later, space), (later, other_yl[1]))[which]
        return remote(src, r3.at[which, rows(k)], r3_s.at[k, which], r3_r.at[k, which], device)

    def step_y(k):
        over_yh(k, yh).start()

    def step_h(k, hop):
        if GATHER[k] == "d":
            if hop == 2:
                over_yh(k, 1 - yh).wait_recv()
            for step in range(1, NZ):
                straight(k, hop - 1, step, 0, yh if hop == 1 else 1 - yh).start()
            return
        if GATHER[k] == "g":
            for direction in (0, 1):
                if (hop - 1, direction) in ring_hops(k):
                    over_z(k, hop - 1, direction, hop - 1).wait_recv()
                if (hop, direction) in ring_hops(k):
                    over_z(k, hop, direction, hop - 1).start()
                if (hop - 1, direction) in ring_hops(k):
                    ring_over_yh(k, hop - 1, direction, yh).start()
            return
        if hop == 1:
            over_yh(k, 1 - yh).wait_recv()
        for direction in (0, 1):
            if hop > 1:
                over_z(k, hop - 1, direction, hop - 1).wait_recv()
            over_z(k, hop, direction, hop - 1).start()

    def step_f(k):
        if GATHER[k] == "d":
            for mirrored in (0, 1):
                for step in range(1, NZ):
                    straight(k, mirrored, step, step, 1 - yh if mirrored else yh).wait_recv()
        elif GATHER[k] == "g":
            over_yh(k, 1 - yh).wait_recv()
            for hop, direction in ring_hops(k):
                ring_over_yh(k, hop, direction, 1 - yh).wait_recv()
        else:
            for direction in (0, 1):
                over_z(k, 4, direction, 4).wait_recv()
        to_core(k, c).start()

    def step_s(k):
        for i in range(4):
            load_model(i).wait()

        def split_rows(t, carry):
            part = m_buf[pl.ds(pl.multiple_of(t * 32, 32), 32), :]
            high = part.astype(BF16)
            low = (part - high.astype(F32)).astype(BF16)
            to = pl.ds(pl.multiple_of(((t % 2) * NZ + t // 4) * 64 + (t // 2) % 2 * 32, 32), 32)
            for d in range(NX):
                for half in (0, 1):
                    lanes = slice(half * 128, half * 128 + 128)
                    columns = slice(half * 512 + d * 128, half * 512 + d * 128 + 128)
                    w_hi[d, to, lanes] = high[:, columns]
                    w_lo[d, to, lanes] = low[:, columns]
            return carry

        lax.fori_loop(0, 32, split_rows, 0)

    def step_t(k):
        to_core(k, 1 - c).wait_recv()

        def block(b, carry):
            columns = pl.ds(pl.multiple_of(b * 128, 128), 128)
            for u in range(SIZES[k]):
                part = kbuf[STARTS[k] + u, pl.ds(2 * b, 2)].reshape(128, 128).T
                high = part.astype(BF16)
                low = (part - high.astype(F32)).astype(BF16)
                kt_hi[u * 128 : (u + 1) * 128, columns] = high
                kt_lo[u * 128 : (u + 1) * 128, columns] = low
            return carry

        lax.fori_loop(0, NZ, block, 0)

    def step_c(k, slot):
        to = (x + (2, 1, 3, 0)[slot]) % NX
        high, low, wide = kt_hi[0 : SIZES[k] * 128], kt_lo[0 : SIZES[k] * 128], w_hi[to]
        acc = jnp.dot(high, wide, preferred_element_type=F32)
        acc = acc + jnp.dot(low, wide, preferred_element_type=F32)
        acc = acc + jnp.dot(high, w_lo[to], preferred_element_type=F32)
        for u in range(SIZES[k]):
            at = (STARTS[k] + u) * UNIT
            for half in (0, 1):
                lanes = slice(half * 128, half * 128 + 128)
                pbuf[slot, half, 0, at : at + UNIT] = acc[u * 128 : u * 128 + UNIT, lanes]
                p1s[slot, half, at : at + UNIT] = acc[u * 128 + UNIT : u * 128 + 2 * UNIT, lanes]
                pbuf[slot, half, 1, at : at + UNIT] = acc[u * 128 + 2 * UNIT : u * 128 + 3 * UNIT, lanes]
        swap_core(k, slot).start()

    def step_x(k, slot):
        swap_core(k, slot).wait_recv()
        for half in (0, 1):
            pbuf[slot, half, 1 - c, rows(k)] += p1r[slot, half, rows(k)]
        if REDUCE[k] == "y":
            over_yl(k, slot).start()

    def step_v(k, slot):
        over_yl(k, slot).wait_recv()
        pbuf[slot, yl, :, rows(k)] += ry[slot, :, rows(k)]

    def step_r1(k):
        if REDUCE[k] == "d":
            far_x(k).start()
            return
        for direction in (0, 1):
            first_x(k, direction).start()

    def step_r2(k):
        for direction in (0, 1):
            if REDUCE[k] == "d":
                second_x(k, direction).start()
                continue
            first_x(k, direction).wait_recv()
            if REDUCE[k] == "y":
                pbuf[1 + direction, yl, direction, rows(k)] += r1[direction, 0, rows(k)]
            else:
                pbuf[1 + direction, direction, :, rows(k)] += r1[direction, :, rows(k)]
            second_x(k, direction).start()

    def step_r3(k):
        for direction in (0, 1):
            second_x(k, direction).wait_recv()
        if REDUCE[k] == "y":
            pbuf[3, yl, :, rows(k)] = pbuf[3, yl, :, rows(k)] + r2[0, 0, :, rows(k)] + r2[1, 0, :, rows(k)]
        else:
            total = pbuf[3, :, :, rows(k)] + r2[0, :, :, rows(k)] + r2[1, :, :, rows(k)]
            if REDUCE[k] == "d":
                far_x(k).wait_recv()
                total = total + r0[:, :, rows(k)]
            pbuf[3, :, :, rows(k)] = total
            last(k, 0).start()

        @pl.when(has_later)
        def _():
            last(k, 1).start()
            if REDUCE[k] != "y":
                last(k, 2).start()

    def step_o(k):
        total = pbuf[3, yl, 0, rows(k)]
        if REDUCE[k] != "y":
            last(k, 0).wait_recv()
            total = total + r3[0, rows(k)]
        out_ref[rows(k)] = total

        @pl.when(has_earlier)
        def _():
            last(k, 1).wait_recv()
            more = r3[1, rows(k)]
            if REDUCE[k] != "y":
                last(k, 2).wait_recv()
                more = more + r3[2, rows(k)]
            out_ref[rows(k)] += more

    def step_d(k):
        over_yh(k, yh).wait_send()
        if GATHER[k] == "d":
            for mirrored in (0, 1):
                for step in range(1, NZ):
                    straight(k, mirrored, step, 0, 1 - yh if mirrored else yh).wait_send()
        elif GATHER[k] == "g":
            for hop, direction in ring_hops(k):
                over_z(k, hop, direction, hop - 1).wait_send()
                ring_over_yh(k, hop, direction, yh).wait_send()
        else:
            for direction in (0, 1):
                for hop in (1, 2, 3, 4):
                    over_z(k, hop, direction, hop - 1).wait_send()
        if REDUCE[k] == "d":
            far_x(k).wait_send()
        for direction in (0, 1):
            if REDUCE[k] != "d":
                first_x(k, direction).wait_send()
            second_x(k, direction).wait_send()
        to_core(k, c).wait_send()
        for slot in range(4):
            swap_core(k, slot).wait_send()
            if REDUCE[k] == "y":
                over_yl(k, slot).wait_send()
        if REDUCE[k] != "y":
            last(k, 0).wait_send()

        @pl.when(has_later)
        def _():
            last(k, 1).wait_send()
            if REDUCE[k] != "y":
                last(k, 2).wait_send()

    steps = {
        "Y": step_y, "F": step_f, "S": step_s, "T": step_t, "R1": step_r1, "R2": step_r2, "R3": step_r3,
        "O": step_o, "D": step_d,
    }
    for hop in (1, 2, 3, 4, 5):
        steps[f"H{hop}"] = functools.partial(step_h, hop=hop)
    for slot in range(4):
        steps[f"C{slot}"] = functools.partial(step_c, slot=slot)
        steps[f"X{slot}"] = functools.partial(step_x, slot=slot)
        steps[f"V{slot}"] = functools.partial(step_v, slot=slot)
    for name, k in ORDER:
        steps[name](k)


def on_device(model, kernels):
    dma, vmem, n = pltpu.SemaphoreType.DMA, pltpu.VMEM, len(SIZES)
    result = pl.pallas_call(
        kernel,
        out_shape=jax.ShapeDtypeStruct((600, 128), F32),
        in_specs=[pl.BlockSpec(memory_space=pl.ANY), pl.BlockSpec(memory_space=pltpu.VMEM)],
        out_specs=pl.BlockSpec(memory_space=pltpu.VMEM),
        scratch_shapes=[
            vmem((1024, 1024), F32),
            vmem((LAGS, 32, 640), F32),
            vmem((UNITS, 2 * NZ, 2, 32, 128), F32),
            vmem((max(SIZES) * 128, 1024), BF16),
            vmem((max(SIZES) * 128, 1024), BF16),
            vmem((NX, 1024, 256), BF16),
            vmem((NX, 1024, 256), BF16),
            vmem((4, 2, 2, 600, 128), F32),
            vmem((4, 2, 600, 128), F32),
            vmem((4, 2, 600, 128), F32),
            vmem((2, 2, 600, 128), F32),
            vmem((2, 2, 600, 128), F32),
            vmem((2, 2, 2, 600, 128), F32),
            vmem((3, 600, 128), F32),
            vmem((4, 2, 600, 128), F32),
            dma((4,)),
            dma((n,)), dma((n,)),
            dma((n, 2, 4)), dma((n, 2, 4)),
            dma((n,)), dma((n,)),
            dma((n, 4)), dma((n, 4)),
            dma((n, 2)), dma((n, 2)),
            dma((n, 2)), dma((n, 2)),
            dma((n, 3)), dma((n, 3)),
            dma((n, 4)), dma((n, 4)),
            dma((n, 2, 4)), dma((n, 2, 4)),
            dma((n, 2, 7)), dma((n, 2, 7)),
        ],
        compiler_params=pltpu.CompilerParams(
            collective_id=0, has_side_effects=True, vmem_limit_bytes=60 * 1024 * 1024
        ),
        name="toeplitz",
    )(model[0], jnp.swapaxes(kernels, 1, 2))
    return result[None]


def solution(mesh):
    return jax.shard_map(
        on_device,
        mesh=mesh,
        in_specs=(P("tm", "space", None), P(None, None, ("space", "tm"))),
        out_specs=P("tm", None, "space"),
        check_vma=False,
    )
```

time: 262 us -> 94.3 us (0.36)
  waiting for transfers between devices: 214 us -> 0 us
  Pallas kernels: 0 us -> 92.5 us
  matrix products: 27.5 us -> 0 us
  between operations: 13.4 us -> 0.01 us
  starting transfers between devices: 4.12 us -> 0 us
    all_gather x1 -> x0, waiting for transfers between devices: 105 us -> none  [on_device(): lax.all_gather(kernels, 'tm', axis=2, tiled=True)]
    pallas_call x0 -> x1, Pallas kernels: none -> 92.5 us  [on_device(): pl.pallas_call(kernel, out_shape=jax.ShapeDtypeStruct((600, 128), F32), i...]
    ppermute x2 -> x0, waiting for transfers between devices: 63.1 us -> none  [passed_along(): return lax.ppermute(block, axis, route)]
    reduce_scatter x1 -> x0, waiting for transfers between devices: 45.3 us -> none  [on_device(): result = lax.psum_scatter(running, 'space', scatter_dimension=1, tiled=True)]
    dot_general x1 -> x0, matrix products: 27.5 us -> none  [on_device(): jnp.einsum('lsp,pc->lsc', lax.all_gather(kernels, 'tm', axis=2, tiled=Tru...]
    ppermute x2 -> x0, starting transfers between devices: 4.08 us -> none  [passed_along(): return lax.ppermute(block, axis, route)]
  transfers between devices with their start and end apart: 4 -> 0, of which waited for: 4 -> 0; matrix products, arithmetic and copies ran while one was open for 0% -> 0% of each run, Pallas kernels for 0% -> 0%
where the time goes in v2:
time: 94.3 us; the launch traced here: 94.2 us
  Pallas kernels  92.5 us (98%)
  local copies, waits for them, and re-layouts  1.7 us (2%)
    pallas_call x1, Pallas kernels, on_device(): pl.pallas_call(kernel, out_shape=jax.ShapeDtypeStruct((600, 128), F32), i...  92.5 us

profile of v2, /device:TPU:32, one launch (start us, length us, event | category | flops | bytes accessed | tf_op | source)
XLA Modules:
  0.0 94.2 jit_solution(11385946789178394867)
XLA Ops:
  0.0 92.5 %toeplitz.1 = f32[600,128]{1,0:T(8,128)} custom-call(f32[1024,1024]{1,0:T(8,128)} %bitcast.3, f32[3,32,600]{2,1,0:T(8,128)} %bitcast.5), custom_call_target="tpu_custom_call" | custom-call | tf_op jit(solution)/shard_map/toeplitz/pallas_call | solution.py:376
  92.5 1.7 %copy.4 = f32[1,600,128]{2,1,0:T(8,128)} copy(f32[1,600,128]{2,1,0:T(8,128)} %bitcast.4) | data formatting | bytes 614400

commit v3 on v2

--- a/solution.py
+++ b/solution.py
@@ -12,29 +12,26 @@
 MESH = pl.DeviceIdType.MESH
 F32, BF16 = jnp.float32, jnp.bfloat16
 
-SIZES = (1, 1, 2, 1, 3, 1, 3, 2, 1)
-GATHER = "gcccgcccc"
-REDUCE = "ddxddyyxx"
+SIZES = (2, 1, 3, 2, 3, 2, 2)
+GATHER = "gcccccc"
+REDUCE = "xxxyxxy"
 ORDER = (
-    ("Y", 0), ("H1", 0), ("Y", 1), ("S", 0), ("Y", 2), ("Y", 3), ("Y", 4), ("H1", 4), ("Y", 5), ("H2", 0), ("H1", 1),
-    ("Y", 6), ("H1", 2), ("Y", 7), ("Y", 8), ("H1", 3), ("H3", 0), ("H2", 1), ("H2", 4), ("H2", 2), ("H4", 0),
-    ("H2", 3), ("H3", 1), ("H3", 4), ("H3", 2), ("H5", 0), ("H3", 3), ("H4", 1), ("H1", 5), ("H4", 4), ("H4", 2),
-    ("F", 0), ("H1", 6), ("F", 1), ("T", 0), ("H4", 3), ("H5", 4), ("C0", 0), ("H2", 5), ("C1", 0), ("F", 2),
-    ("C2", 0), ("H1", 7), ("C3", 0), ("T", 1), ("X0", 0), ("R1", 0), ("X1", 0), ("C0", 1), ("H2", 6), ("C1", 1),
-    ("C2", 1), ("F", 3), ("X2", 0), ("R2", 0), ("X3", 0), ("C3", 1), ("F", 4), ("X0", 1), ("X1", 1), ("T", 2),
-    ("H3", 5), ("R1", 1), ("X2", 1), ("X3", 1), ("C0", 2), ("H2", 7), ("C1", 2), ("R2", 1), ("C2", 2), ("H3", 6),
-    ("C3", 2), ("R3", 0), ("X0", 2), ("R1", 2), ("X1", 2), ("T", 3), ("X2", 2), ("C0", 3), ("H4", 5), ("X3", 2),
-    ("H1", 8), ("C1", 3), ("C2", 3), ("H3", 7), ("C3", 3), ("X0", 3), ("R1", 3), ("T", 4), ("H4", 6), ("R3", 1),
-    ("X1", 3), ("X2", 3), ("R2", 3), ("F", 5), ("X3", 3), ("C0", 4), ("H2", 8), ("O", 0), ("R2", 2), ("C1", 4),
-    ("H4", 7), ("C2", 4), ("F", 6), ("X0", 4), ("C3", 4), ("R3", 3), ("H3", 8), ("R1", 4), ("X1", 4), ("X2", 4),
-    ("O", 1), ("T", 5), ("C0", 5), ("F", 7), ("C1", 5), ("C2", 5), ("C3", 5), ("R3", 2), ("X3", 4), ("X0", 5),
-    ("T", 6), ("H4", 8), ("X1", 5), ("X2", 5), ("X3", 5), ("C0", 6), ("O", 3), ("R2", 4), ("C1", 6), ("C2", 6),
-    ("X0", 6), ("C3", 6), ("F", 8), ("X1", 6), ("V0", 5), ("T", 7), ("O", 2), ("V1", 5), ("X2", 6), ("X3", 6),
-    ("C0", 7), ("R1", 5), ("V2", 5), ("C1", 7), ("V3", 5), ("C2", 7), ("X0", 7), ("R1", 7), ("C3", 7), ("R3", 4),
-    ("V0", 6), ("R1", 6), ("X1", 7), ("X2", 7), ("T", 8), ("C0", 8), ("X3", 7), ("R2", 5), ("C1", 8), ("C2", 8),
-    ("C3", 8), ("V1", 6), ("X0", 8), ("R1", 8), ("D", 0), ("R2", 7), ("X1", 8), ("X2", 8), ("D", 1), ("X3", 8),
-    ("D", 2), ("D", 3), ("V2", 6), ("R3", 5), ("R2", 6), ("V3", 6), ("R3", 7), ("R2", 8), ("R3", 6), ("O", 4),
-    ("D", 4), ("O", 5), ("D", 5), ("R3", 8), ("O", 7), ("O", 6), ("D", 6), ("D", 7), ("O", 8), ("D", 8),
+    ("Y", 0), ("H1", 0), ("Y", 1), ("S", 0), ("Y", 2), ("Y", 3), ("Y", 4), ("H2", 0), ("H1", 1), ("Y", 5), ("H1", 2),
+    ("Y", 6), ("H3", 0), ("H1", 3), ("H2", 1), ("H2", 2), ("H4", 0), ("H2", 3), ("H3", 1), ("H3", 2), ("H5", 0),
+    ("H1", 4), ("H3", 3), ("F", 0), ("H4", 1), ("H4", 2), ("H2", 4), ("T", 0), ("C0", 0), ("H4", 3), ("C1", 0),
+    ("F", 1), ("H1", 6), ("C2", 0), ("F", 2), ("X0", 0), ("R1", 0), ("C3", 0), ("H1", 5), ("X1", 0), ("T", 1),
+    ("X2", 0), ("C0", 1), ("H3", 4), ("C1", 1), ("F", 3), ("C2", 1), ("C3", 1), ("T", 2), ("R2", 0), ("H2", 6),
+    ("X3", 0), ("X0", 1), ("R1", 1), ("X1", 1), ("C0", 2), ("H2", 5), ("X2", 1), ("X3", 1), ("C1", 2), ("H4", 4),
+    ("C2", 2), ("X0", 2), ("R1", 2), ("C3", 2), ("H3", 6), ("X1", 2), ("T", 3), ("R3", 0), ("H3", 5), ("X3", 2),
+    ("X2", 2), ("C0", 3), ("F", 4), ("C1", 3), ("R2", 1), ("C2", 3), ("X0", 3), ("H4", 6), ("C3", 3), ("R2", 2),
+    ("H4", 5), ("T", 4), ("X1", 3), ("X2", 3), ("X3", 3), ("R3", 1), ("F", 6), ("O", 0), ("C0", 4), ("V0", 3),
+    ("R1", 3), ("F", 5), ("C1", 4), ("C2", 4), ("X0", 4), ("R1", 4), ("C3", 4), ("R3", 2), ("V1", 3), ("X1", 4),
+    ("X2", 4), ("T", 5), ("V2", 3), ("X3", 4), ("C0", 5), ("R2", 3), ("C1", 5), ("V3", 3), ("C2", 5), ("R2", 4),
+    ("X0", 5), ("C3", 5), ("X1", 5), ("T", 6), ("R1", 5), ("X2", 5), ("O", 1), ("C0", 6), ("R3", 3), ("X3", 5),
+    ("C1", 6), ("C2", 6), ("X0", 6), ("C3", 6), ("O", 2), ("X1", 6), ("D", 0), ("X2", 6), ("D", 1), ("D", 2),
+    ("X3", 6), ("R3", 4), ("O", 3), ("D", 3), ("V0", 6), ("R1", 6), ("R2", 5), ("V1", 6), ("V2", 6), ("R2", 6),
+    ("V3", 6), ("R3", 5), ("R3", 6), ("D", 4), ("D", 5), ("D", 6), ("E", 0), ("E", 1), ("E", 2), ("E", 3), ("O", 4),
+    ("O", 5), ("O", 6), ("E", 4), ("E", 5), ("E", 6),
 )
 STARTS = tuple(sum(SIZES[:k]) for k in range(len(SIZES)))
 
@@ -348,6 +345,8 @@
             swap_core(k, slot).wait_send()
             if REDUCE[k] == "y":
                 over_yl(k, slot).wait_send()
+
+    def step_e(k):
         if REDUCE[k] != "y":
             last(k, 0).wait_send()
 
@@ -359,7 +358,7 @@
 
     steps = {
         "Y": step_y, "F": step_f, "S": step_s, "T": step_t, "R1": step_r1, "R2": step_r2, "R3": step_r3,
-        "O": step_o, "D": step_d,
+        "O": step_o, "D": step_d, "E": step_e,
     }
     for hop in (1, 2, 3, 4, 5):
         steps[f"H{hop}"] = functools.partial(step_h, hop=hop)

time: 94.3 us -> 94.5 us (level)
  no operation moved by 1% of the time
where the time goes in v3:
time: 94.5 us; the launch traced here: 94.4 us
  Pallas kernels  92.7 us (98%)
  local copies, waits for them, and re-layouts  1.7 us (2%)
    pallas_call x1, Pallas kernels, on_device(): pl.pallas_call(kernel, out_shape=jax.ShapeDtypeStruct((600, 128), F32), i...  92.7 us

profile of v3, /device:TPU:32, one launch (start us, length us, event | category | flops | bytes accessed | tf_op | source)
XLA Modules:
  0.0 94.4 jit_solution(3167624685267200705)
XLA Ops:
  0.0 92.7 %toeplitz.1 = f32[600,128]{1,0:T(8,128)} custom-call(f32[1024,1024]{1,0:T(8,128)} %bitcast.3, f32[3,32,600]{2,1,0:T(8,128)} %bitcast.5), custom_call_target="tpu_custom_call" | custom-call | tf_op jit(solution)/shard_map/toeplitz/pallas_call | solution.py:375
  92.7 1.7 %copy.4 = f32[1,600,128]{2,1,0:T(8,128)} copy(f32[1,600,128]{2,1,0:T(8,128)} %bitcast.4) | data formatting | bytes 614400

commit v4 on v3

--- a/solution.py
+++ b/solution.py
@@ -12,33 +12,35 @@
 MESH = pl.DeviceIdType.MESH
 F32, BF16 = jnp.float32, jnp.bfloat16
 
-SIZES = (2, 1, 3, 2, 3, 2, 2)
-GATHER = "gcccccc"
-REDUCE = "xxxyxxy"
+SIZES = (1, 2, 2, 1, 3, 3, 2, 1)
+GATHER = "gcccgccc"
+REDUCE = "dxxyxyxx"
 ORDER = (
-    ("Y", 0), ("H1", 0), ("Y", 1), ("S", 0), ("Y", 2), ("Y", 3), ("Y", 4), ("H2", 0), ("H1", 1), ("Y", 5), ("H1", 2),
-    ("Y", 6), ("H3", 0), ("H1", 3), ("H2", 1), ("H2", 2), ("H4", 0), ("H2", 3), ("H3", 1), ("H3", 2), ("H5", 0),
-    ("H1", 4), ("H3", 3), ("F", 0), ("H4", 1), ("H4", 2), ("H2", 4), ("T", 0), ("C0", 0), ("H4", 3), ("C1", 0),
-    ("F", 1), ("H1", 6), ("C2", 0), ("F", 2), ("X0", 0), ("R1", 0), ("C3", 0), ("H1", 5), ("X1", 0), ("T", 1),
-    ("X2", 0), ("C0", 1), ("H3", 4), ("C1", 1), ("F", 3), ("C2", 1), ("C3", 1), ("T", 2), ("R2", 0), ("H2", 6),
-    ("X3", 0), ("X0", 1), ("R1", 1), ("X1", 1), ("C0", 2), ("H2", 5), ("X2", 1), ("X3", 1), ("C1", 2), ("H4", 4),
-    ("C2", 2), ("X0", 2), ("R1", 2), ("C3", 2), ("H3", 6), ("X1", 2), ("T", 3), ("R3", 0), ("H3", 5), ("X3", 2),
-    ("X2", 2), ("C0", 3), ("F", 4), ("C1", 3), ("R2", 1), ("C2", 3), ("X0", 3), ("H4", 6), ("C3", 3), ("R2", 2),
-    ("H4", 5), ("T", 4), ("X1", 3), ("X2", 3), ("X3", 3), ("R3", 1), ("F", 6), ("O", 0), ("C0", 4), ("V0", 3),
-    ("R1", 3), ("F", 5), ("C1", 4), ("C2", 4), ("X0", 4), ("R1", 4), ("C3", 4), ("R3", 2), ("V1", 3), ("X1", 4),
-    ("X2", 4), ("T", 5), ("V2", 3), ("X3", 4), ("C0", 5), ("R2", 3), ("C1", 5), ("V3", 3), ("C2", 5), ("R2", 4),
-    ("X0", 5), ("C3", 5), ("X1", 5), ("T", 6), ("R1", 5), ("X2", 5), ("O", 1), ("C0", 6), ("R3", 3), ("X3", 5),
-    ("C1", 6), ("C2", 6), ("X0", 6), ("C3", 6), ("O", 2), ("X1", 6), ("D", 0), ("X2", 6), ("D", 1), ("D", 2),
-    ("X3", 6), ("R3", 4), ("O", 3), ("D", 3), ("V0", 6), ("R1", 6), ("R2", 5), ("V1", 6), ("V2", 6), ("R2", 6),
-    ("V3", 6), ("R3", 5), ("R3", 6), ("D", 4), ("D", 5), ("D", 6), ("E", 0), ("E", 1), ("E", 2), ("E", 3), ("O", 4),
-    ("O", 5), ("O", 6), ("E", 4), ("E", 5), ("E", 6),
+    ("Y", 0), ("Y", 1), ("H1", 0), ("S", 0), ("Y", 2), ("Y", 3), ("Y", 4), ("H1", 4), ("Y", 5), ("H2", 0), ("H1", 1),
+    ("Y", 6), ("H1", 2), ("Y", 7), ("H1", 3), ("H3", 0), ("H2", 4), ("H2", 1), ("H1", 7), ("H2", 3), ("H4", 0),
+    ("H2", 2), ("H3", 1), ("H3", 4), ("H5", 0), ("H3", 3), ("H3", 2), ("H4", 1), ("H1", 5), ("F", 0), ("H4", 3),
+    ("H4", 2), ("H4", 4), ("F", 1), ("T", 0), ("H1", 6), ("C0", 0), ("C1", 0), ("C2", 0), ("H2", 5), ("C3", 0),
+    ("F", 3), ("T", 1), ("F", 2), ("X0", 0), ("R1", 0), ("X1", 0), ("X2", 0), ("R2", 0), ("H5", 4), ("X3", 0),
+    ("C0", 1), ("H2", 7), ("C1", 1), ("H2", 6), ("C2", 1), ("C3", 1), ("X0", 1), ("R1", 1), ("X1", 1), ("T", 2),
+    ("H3", 5), ("X2", 1), ("C0", 2), ("F", 4), ("X3", 1), ("C1", 2), ("H3", 6), ("R3", 0), ("C2", 2), ("X0", 2),
+    ("R1", 2), ("C3", 2), ("H3", 7), ("R2", 1), ("T", 3), ("C0", 3), ("H4", 5), ("X2", 2), ("X1", 2), ("C1", 3),
+    ("X3", 2), ("C2", 3), ("C3", 3), ("H4", 6), ("T", 4), ("H4", 7), ("O", 0), ("R2", 2), ("X1", 3), ("C0", 4),
+    ("F", 5), ("X0", 3), ("X2", 3), ("X3", 3), ("C1", 4), ("F", 6), ("R3", 1), ("X0", 4), ("R1", 4), ("C2", 4),
+    ("F", 7), ("V1", 3), ("C3", 4), ("T", 5), ("R3", 2), ("X1", 4), ("V0", 3), ("R1", 3), ("X2", 4), ("V2", 3),
+    ("V3", 3), ("C0", 5), ("X3", 4), ("C1", 5), ("R2", 4), ("C2", 5), ("X0", 5), ("O", 1), ("C3", 5), ("R2", 3),
+    ("X1", 5), ("X2", 5), ("T", 6), ("O", 2), ("C0", 6), ("X3", 5), ("C1", 6), ("C2", 6), ("C3", 6), ("X0", 6),
+    ("R1", 6), ("V0", 5), ("R1", 5), ("T", 7), ("R3", 4), ("X2", 6), ("C0", 7), ("C1", 7), ("X1", 6), ("V1", 5),
+    ("X3", 6), ("C2", 7), ("R3", 3), ("X0", 7), ("R1", 7), ("C3", 7), ("X1", 7), ("D", 0), ("D", 1), ("R2", 6),
+    ("X2", 7), ("D", 2), ("V2", 5), ("X3", 7), ("R2", 5), ("R2", 7), ("V3", 5), ("R3", 6), ("O", 4), ("R3", 5),
+    ("O", 3), ("D", 3), ("D", 4), ("R3", 7), ("D", 5), ("D", 6), ("D", 7), ("E", 0), ("E", 1), ("E", 2), ("E", 3),
+    ("E", 4), ("O", 6), ("O", 5), ("O", 7), ("E", 5), ("E", 6), ("E", 7),
 )
 STARTS = tuple(sum(SIZES[:k]) for k in range(len(SIZES)))
 
 
 def kernel(
     m_hbm, k_ref, out_ref,
-    m_buf, k_pad, kbuf, kt_hi, kt_lo, w_hi, w_lo, pbuf, p1s, p1r, r0, r1, r2, r3, ry,
+    m_buf, k_pad, kbuf, kt, w_hi, w_lo, pbuf, p1s, p1r, r0, r1, r2, r3, ry,
     m_sem, ky_s, ky_r, kz_s, kz_r, kf_s, kf_r, p1_s, p1_rs, r1_s, r1_r, r2_s, r2_r, r3_s, r3_r, ry_s, ry_r, kg_s, kg_r, kd_s, kd_r,
 ):
     tm, space = lax.axis_index("tm"), lax.axis_index("space")
@@ -234,18 +236,18 @@
                 part = kbuf[STARTS[k] + u, pl.ds(2 * b, 2)].reshape(128, 128).T
                 high = part.astype(BF16)
                 low = (part - high.astype(F32)).astype(BF16)
-                kt_hi[u * 128 : (u + 1) * 128, columns] = high
-                kt_lo[u * 128 : (u + 1) * 128, columns] = low
+                kt[u * 128 : (u + 1) * 128, columns] = high
+                kt[(SIZES[k] + u) * 128 : (SIZES[k] + u + 1) * 128, columns] = low
             return carry
 
         lax.fori_loop(0, NZ, block, 0)
 
     def step_c(k, slot):
         to = (x + (2, 1, 3, 0)[slot]) % NX
-        high, low, wide = kt_hi[0 : SIZES[k] * 128], kt_lo[0 : SIZES[k] * 128], w_hi[to]
-        acc = jnp.dot(high, wide, preferred_element_type=F32)
-        acc = acc + jnp.dot(low, wide, preferred_element_type=F32)
-        acc = acc + jnp.dot(high, w_lo[to], preferred_element_type=F32)
+        size = SIZES[k] * 128
+        both = jnp.dot(kt[0 : 2 * size], w_hi[to], preferred_element_type=F32)
+        acc = both[0:size] + both[size : 2 * size]
+        acc = acc + jnp.dot(kt[0:size], w_lo[to], preferred_element_type=F32)
         for u in range(SIZES[k]):
             at = (STARTS[k] + u) * UNIT
             for half in (0, 1):
@@ -381,8 +383,7 @@
             vmem((1024, 1024), F32),
             vmem((LAGS, 32, 640), F32),
             vmem((UNITS, 2 * NZ, 2, 32, 128), F32),
-            vmem((max(SIZES) * 128, 1024), BF16),
-            vmem((max(SIZES) * 128, 1024), BF16),
+            vmem((max(SIZES) * 256, 1024), BF16),
             vmem((NX, 1024, 256), BF16),
             vmem((NX, 1024, 256), BF16),
             vmem((4, 2, 2, 600, 128), F32),

time: 94.5 us -> 93.3 us (0.987)
  Pallas kernels: 92.7 us -> 91.5 us
    pallas_call x1, Pallas kernels: 92.7 us -> 91.5 us  [on_device(): pl.pallas_call(kernel, out_shape=jax.ShapeDtypeStruct((600, 128), F32), i...]
where the time goes in v4:
time: 93.3 us; the launch traced here: 93.2 us
  Pallas kernels  91.5 us (98%)
  local copies, waits for them, and re-layouts  1.7 us (2%)
    pallas_call x1, Pallas kernels, on_device(): pl.pallas_call(kernel, out_shape=jax.ShapeDtypeStruct((600, 128), F32), i...  91.5 us

profile of v4, /device:TPU:32, one launch (start us, length us, event | category | flops | bytes accessed | tf_op | source)
XLA Modules:
  0.0 93.2 jit_solution(15989957772143404402)
XLA Ops:
  0.0 91.5 %toeplitz.1 = f32[600,128]{1,0:T(8,128)} custom-call(f32[1024,1024]{1,0:T(8,128)} %bitcast.3, f32[3,32,600]{2,1,0:T(8,128)} %bitcast.5), custom_call_target="tpu_custom_call" | custom-call | tf_op jit(solution)/shard_map/toeplitz/pallas_call | solution.py:377
  91.5 1.7 %copy.4 = f32[1,600,128]{2,1,0:T(8,128)} copy(f32[1,600,128]{2,1,0:T(8,128)} %bitcast.4) | data formatting | bytes 614400
